TPU v7x, 256 devices: a whole 4x4x8 slice. The times are simulated.
256 devices in a mesh: depth: 32 (over z, x), replica: 8 (over y, core).
Axes of the slice: x: 4, y: 4, z: 8, core: 2. Of those that a mesh axis runs over, the one named last changes fastest.
Arguments:
- volume: bfloat16 [8, 64, 16, 16, 256], P('replica', 'depth'), may hold values from -8 to 8, as said below
- cotangent: bfloat16 [8, 64, 16, 16, 256], P('replica', 'depth'), may hold values from -8 to 8, as said below
- kernel: bfloat16 [3, 3, 3, 256, 256], replicated, may hold values from -0.078125 to 0.078125
Outputs:
- grad_volume: bfloat16 [8, 64, 16, 16, 256], P('replica', 'depth')
- merged_grad: float32 [6912, 256], P('depth', 'replica')
Inputs may be any that keep to these rules, and one draw needn't show every extreme that they name: `volume`: input fields, independent across voxels and channels. cotangent entries, independent across voxels and channels.
All inputs are finite; a program needn't handle non-finite values.
Results may differ from a plain program's by a relative error of at most 0.0019.
The roundings to bfloat16 on the way count: a program that leaves them out, or rounds other values in their place, can miss the bound.
Values may be sent and summed in bfloat16 or wider, within the bound.
A program may use at most 128 MiB of HBM per device.

v0:
```python
import math

import jax
import jax.numpy as jnp
from jax import lax
from jax.sharding import Mesh
from jax.sharding import PartitionSpec as P

DEPTH = ("depth_0", "depth_1")


epsilon = 1e-06


def with_halo(x, sides, width):
    for axis, dim in sides:
        count, length = (lax.axis_size(axis), x.shape[dim])
        up = [(i, (i + 1) % count) for i in range(count - 1)]
        down = [(j, i) for i, j in up]
        last = lax.slice_in_dim(x, length - width, length, axis=dim)
        first = lax.slice_in_dim(x, 0, width, axis=dim)
        before = lax.ppermute(last, axis, up)
        after = lax.ppermute(first, axis, down)
        x = jnp.concatenate([before, x, after], axis=dim)
    return x


def summed_rows(x, axes, dim):
    for axis in axes:
        x = lax.psum_scatter(x, axis, scatter_dimension=dim, tiled=True)
    return x


def from_partner(block, axis, apart):
    count = lax.axis_size(axis)
    route = []
    for low in range(count):
        high = low | 1 << apart
        if high != low and high < count:
            route += [(low, high), (high, low)]
    return lax.ppermute(block, axis, route)


def sent_to_all(x, axis):
    copies = jnp.broadcast_to(x, (lax.axis_size(axis), *x.shape))
    return lax.all_to_all(copies, axis, split_axis=0, concat_axis=0, tiled=True)


def taken_together(x, axis):
    return sent_to_all(x, axis).sum(axis=0)


def packed_total(arrays, axis):
    ends = [0]
    for a in arrays:
        ends.append(ends[-1] + a.size)
    total = taken_together(jnp.concatenate([a.ravel() for a in arrays]), axis)
    return tuple((total[b:e].reshape(a.shape) for a, b, e in zip(arrays, ends, ends[1:])))


def columns(padded, planes, height, breadth):
    pieces = []
    for depth_off in range(3):
        for row_off in range(3):
            for col_off in range(3):
                pieces.append(
                    padded[
                        depth_off : depth_off + planes,
                        row_off : row_off + height,
                        col_off : col_off + breadth,
                        :,
                    ]
                )
    joined = jnp.concatenate(pieces, -1)
    return joined.reshape(planes * height * breadth, joined.shape[-1])


def silu_slope(preact, upstream):
    sigmoid_val = jax.nn.sigmoid(preact)
    return (
        upstream.astype(jnp.float32) * sigmoid_val * (1.0 + preact * (1.0 - sigmoid_val))
    ).astype(jnp.bfloat16)


def adasum_pair(own_grad, partner_grad, inner_prod, own_norm, partner_norm):
    return (1.0 - inner_prod / (2.0 * (own_norm + epsilon))) * own_grad + (
        1.0 - inner_prod / (2.0 * (partner_norm + epsilon))
    ) * partner_grad


def shards(volume, cotangent, kernel):
    own_field = volume[0]
    upstream = cotangent[0]
    planes, height, breadth, channels = own_field.shape
    voxel_count = planes * height * breadth
    kernel_flat = kernel.reshape(27 * channels, channels)
    kernel_flip = kernel[::-1, ::-1, ::-1].transpose(0, 1, 2, 4, 3).reshape(27 * channels, channels)
    border = ((0, 0), (1, 1), (1, 1), (0, 0))
    contract = (((0,), (0,)), ((), ()))
    extended = with_halo(own_field, ((DEPTH, 0),), 1)
    own_columns = columns(jnp.pad(extended, border), planes, height, breadth)
    preact = jnp.dot(own_columns, kernel_flat, preferred_element_type=jnp.float32)
    pre_grad = silu_slope(preact, upstream.reshape(voxel_count, channels))
    local_grad = lax.dot_general(
        own_columns, pre_grad, contract, preferred_element_type=jnp.float32
    )
    grad_extended = with_halo(pre_grad.reshape(planes, height, breadth, channels), ((DEPTH, 0),), 1)
    grad_columns = columns(jnp.pad(grad_extended, border), planes, height, breadth)
    grad_field = jnp.dot(grad_columns, kernel_flip, preferred_element_type=jnp.float32).astype(
        jnp.bfloat16
    )
    grad_field = grad_field.reshape(1, planes, height, breadth, channels)
    factor = 1.0 / math.sqrt(voxel_count * lax.axis_size(DEPTH))
    level_count = lax.axis_size("replica").bit_length() - 1
    merged = summed_rows(local_grad, DEPTH, 0) * factor
    for bit_index in range(level_count):
        partner_grad = from_partner(merged, "replica", bit_index)
        inner_prod, own_norm, partner_norm = packed_total(
            (
                jnp.sum(merged * partner_grad),
                jnp.sum(merged * merged),
                jnp.sum(partner_grad * partner_grad),
            ),
            DEPTH,
        )
        merged = adasum_pair(merged, partner_grad, inner_prod, own_norm, partner_norm)
    column_count = channels // lax.axis_size("replica")
    column_start = lax.axis_index("replica") * column_count
    merged = lax.dynamic_slice_in_dim(merged, column_start, column_count, 1)
    return (grad_field, merged)


def solution(mesh):
    finer = Mesh(
        mesh.devices.reshape(8, 4, mesh.shape["replica"]), ("depth_0", "depth_1", "replica")
    )
    return jax.shard_map(
        shards,
        mesh=finer,
        in_specs=(
            P("replica", DEPTH, None, None, None),
            P("replica", DEPTH, None, None, None),
            P(),
        ),
        out_specs=(P("replica", DEPTH, None, None, None), P(DEPTH, "replica")),
        check_vma=False,
    )
```

profile of v0, /device:TPU:8, one launch (start us, length us, event | category | flops | bytes accessed | tf_op | source)
XLA Modules:
  0.0 243.9 jit_solution(5812653644792932661)
XLA Ops:
  8.2 3.4 %collective-permute-start = (bf16[1,16,16,256]{3,2,1,0:T(8,128)(2,1)S(1)}, bf16[1,16,16,256]{3,2,1,0:T(8,128)(2,1)S(1)}, u32[]{:S(2)}, u32[]{:S(2)}) collective-permute-start(bf16[1,16,16,256]{3,2,1,0:T(8,128)(2,1)S(1)} %get-tuple-element.75), channel_id=1, source_target_pairs={{0,8},{8,16},{16,24},{24,32},{32,40},{40,48},{48,56},{56,64},{64,7... | collective-permute-start | bytes 393224 | tf_op jit(solution)/shard_map/ppermute | solution.py:22
  14.3 4.1 %collective-permute-done.1 = bf16[1,16,16,256]{3,2,1,0:T(8,128)(2,1)S(1)} collective-permute-done((bf16[1,16,16,256]{3,2,1,0:T(8,128)(2,1)S(1)}, bf16[1,16,16,256]{3,2,1,0:T(8,128)(2,1)S(1)}, u32[]{:S(2)}, u32[]{:S(2)}) %collective-permute-start.1) | collective-permute-done | bytes 131104 | tf_op jit(solution)/shard_map/ppermute | solution.py:23
  22.7 2.1 fusion.5
  25.6 5.2 %fusion.6 = f32[6912,256]{1,0:T(8,128)} fusion(bf16[512,6912]{1,0:T(8,128)(2,1)S(1)} %constant_dynamic-update-slice_fusion, bf16[512,256]{1,0:T(8,128)(2,1)S(1)} %bitcast.149, f32[512,256]{1,0:T(8,128)S(1)} %get-tuple-element.87), kind=kOutput, calls=%fused_computation.16 | convolution fusion | flops 1813250048 | bytes 14942208 | tf_op jit(solution)/shard_map/dot_general | solution.py:104
  31.6 4.0 %collective-permute-start.2 = (bf16[1,16,16,256]{3,2,1,0:T(8,128)(2,1)}, bf16[1,16,16,256]{3,2,1,0:T(8,128)(2,1)}, u32[]{:S(2)}, u32[]{:S(2)}) collective-permute-start(bf16[1,16,16,256]{3,2,1,0:T(8,128)(2,1)} %bitcast.32), channel_id=1, source_target_pairs={{0,8},{8,16},{16,24},{24,32},{32,40},{40,48},{48,56},{56,64},{64,7... | collective-permute-start | bytes 393224 | tf_op jit(solution)/shard_map/ppermute | solution.py:22
  36.9 4.3 %copy.15 = bf16[3,3,3,256,256]{3,4,2,1,0:T(8,128)(2,1)S(1)} copy(bf16[3,3,3,256,256]{4,3,2,1,0:T(8,128)(2,1)} %param.5) | data formatting | bytes 7077888 | tf_op args[2]
  41.2 2.0 rev.3
  50.4 2.3 fusion.12
  52.7 65.7 %reduce-scatter.3.cloned.1.call-done = f32[864,256]{1,0:T(8,128)} async-done(((f32[6912,256]{1,0:T(8,128)}), f32[864,256]{1,0:T(8,128)}) %reduce-scatter.3.cloned.1.call-update) | async-done | bytes 884752 | tf_op jit(solution)/shard_map/reduce_scatter | solution.py:30
  120.7 1.9 constant_dynamic-update-slice_fusion.44
  129.4 2.0 fusion.8
  139.1 6.0 %reduce-scatter.5.cloned.1.call-done = f32[216,256]{1,0:T(8,128)} async-done(((f32[864,256]{1,0:T(8,128)}), f32[216,256]{1,0:T(8,128)}) %reduce-scatter.5.cloned.1.call-update) | async-done | bytes 221200 | tf_op jit(solution)/shard_map/reduce_scatter | solution.py:30
  152.0 2.0 pad_maximum_fusion.4
  154.6 8.3 %all-to-all-start = ((f32[32,1,3]{2,1,0:T(1,128)}), f32[32,1,3]{2,1,0:T(1,128)S(1)}, u32[]{:S(2)}, u32[]{:S(2)}) async-start(f32[32,1,3]{2,1,0:T(1,128)} %broadcast_in_dim.9), calls=%async_computation.2 | async-start | bytes 32768 | tf_op jit(solution)/shard_map/all_to_all | solution.py:46
  164.6 8.0 %all-to-all-done = f32[32,1,3]{2,1,0:T(1,128)S(1)} async-done(((f32[32,1,3]{2,1,0:T(1,128)}), f32[32,1,3]{2,1,0:T(1,128)S(1)}, u32[]{:S(2)}, u32[]{:S(2)}) %all-to-all-start) | async-done | bytes 416 | tf_op jit(solution)/shard_map/all_to_all | solution.py:46
  182.3 2.4 collective-permute-done.5
  185.5 2.0 pad_maximum_fusion.5
  188.1 3.8 %all-to-all-start.1 = ((f32[32,1,3]{2,1,0:T(1,128)}), f32[32,1,3]{2,1,0:T(1,128)S(1)}, u32[]{:S(2)}, u32[]{:S(2)}) async-start(f32[32,1,3]{2,1,0:T(1,128)} %broadcast_in_dim.10), calls=%async_computation.3 | async-start | bytes 32768 | tf_op jit(solution)/shard_map/all_to_all | solution.py:46
  193.7 8.0 %all-to-all-done.1 = f32[32,1,3]{2,1,0:T(1,128)S(1)} async-done(((f32[32,1,3]{2,1,0:T(1,128)}), f32[32,1,3]{2,1,0:T(1,128)S(1)}, u32[]{:S(2)}, u32[]{:S(2)}) %all-to-all-start.1) | async-done | bytes 416 | tf_op jit(solution)/shard_map/all_to_all | solution.py:46
  207.3 2.4 collective-permute-start.6
  215.8 2.1 pad_maximum_fusion.6
  218.5 3.8 %all-to-all-start.2 = ((f32[32,1,3]{2,1,0:T(1,128)}), f32[32,1,3]{2,1,0:T(1,128)S(1)}, u32[]{:S(2)}, u32[]{:S(2)}) async-start(f32[32,1,3]{2,1,0:T(1,128)} %broadcast_in_dim.11), calls=%async_computation.4 | async-start | bytes 32768 | tf_op jit(solution)/shard_map/all_to_all | solution.py:46
  222.3 5.7 %convolution_convert_fusion = bf16[512,256]{1,0:T(8,128)(2,1)} fusion(bf16[512,6912]{1,0:T(8,128)(2,1)} %constant_dynamic-update-slice_fusion.27, bf16[6912,256]{1,0:T(8,128)(2,1)S(1)} %bitcast.93), kind=kOutput, calls=%fused_computation.7 | convolution fusion | flops 1812070400 | bytes 10878976 | tf_op jit(solution)/shard_map/dot_general | solution.py:109
  228.0 4.0 %all-to-all-done.2 = f32[32,1,3]{2,1,0:T(1,128)S(1)} async-done(((f32[32,1,3]{2,1,0:T(1,128)}), f32[32,1,3]{2,1,0:T(1,128)S(1)}, u32[]{:S(2)}, u32[]{:S(2)}) %all-to-all-start.2) | async-done | bytes 416 | tf_op jit(solution)/shard_map/all_to_all | solution.py:46
  (115 shorter events, 66.0 us)
Async XLA Ops:
  7.2 111.2 %reduce-scatter.3.cloned.1.call-start = ((), (), s32[]{:S(2)}) async-start(), calls=%async_computation.5 | async-start | bytes 7962624 | tf_op jit(solution)/shard_map/reduce_scatter | solution.py:30
  8.2 6.1 %collective-permute-start = (bf16[1,16,16,256]{3,2,1,0:T(8,128)(2,1)S(1)}, bf16[1,16,16,256]{3,2,1,0:T(8,128)(2,1)S(1)}, u32[]{:S(2)}, u32[]{:S(2)}) collective-permute-start(bf16[1,16,16,256]{3,2,1,0:T(8,128)(2,1)S(1)} %get-tuple-element.75), channel_id=1, source_target_pairs={{0,8},{8,16},{16,24},{24,32},{32,40},{40,48},{48,56},{56,64},{64,7... | collective-permute-start | bytes 393224 | tf_op jit(solution)/shard_map/ppermute | solution.py:22
  11.6 6.9 %collective-permute-start.1 = (bf16[1,16,16,256]{3,2,1,0:T(8,128)(2,1)S(1)}, bf16[1,16,16,256]{3,2,1,0:T(8,128)(2,1)S(1)}, u32[]{:S(2)}, u32[]{:S(2)}) collective-permute-start(bf16[1,16,16,256]{3,2,1,0:T(8,128)(2,1)S(1)} %get-tuple-element.76), channel_id=1, source_target_pairs={{8,0},{16,8},{24,16},{32,24},{40,32},{48,40},{56,48},{64,56},{72,6... | collective-permute-start | bytes 393224 | tf_op jit(solution)/shard_map/ppermute | solution.py:23
  19.8 1.0 copy-start
  20.7 2.0 copy-start.1
  20.7 2.0 copy-start.11
  24.8 0.8 copy-start.9
  24.8 6.0 %copy-start.3 = (bf16[512,256]{1,0:T(8,128)(2,1)}, bf16[512,256]{1,0:T(8,128)(2,1)S(1)}, u32[]{:S(2)}) copy-start(bf16[512,256]{1,0:T(8,128)(2,1)S(1)} %get-tuple-element.86) | copy-start | bytes 786436
  30.8 114.3 %reduce-scatter.5.cloned.1.call-start = ((), (), s32[]{:S(2)}) async-start(), calls=%async_computation.6 | async-start | bytes 1105920 | tf_op jit(solution)/shard_map/reduce_scatter | solution.py:30
  31.6 11.6 %collective-permute-start.2 = (bf16[1,16,16,256]{3,2,1,0:T(8,128)(2,1)}, bf16[1,16,16,256]{3,2,1,0:T(8,128)(2,1)}, u32[]{:S(2)}, u32[]{:S(2)}) collective-permute-start(bf16[1,16,16,256]{3,2,1,0:T(8,128)(2,1)} %bitcast.32), channel_id=1, source_target_pairs={{0,8},{8,16},{16,24},{24,32},{32,40},{40,48},{48,56},{56,64},{64,7... | collective-permute-start | bytes 393224 | tf_op jit(solution)/shard_map/ppermute | solution.py:22
  35.6 7.5 %collective-permute-start.3 = (bf16[1,16,16,256]{3,2,1,0:T(8,128)(2,1)}, bf16[1,16,16,256]{3,2,1,0:T(8,128)(2,1)}, u32[]{:S(2)}, u32[]{:S(2)}) collective-permute-start(bf16[1,16,16,256]{3,2,1,0:T(8,128)(2,1)} %bitcast.34), channel_id=1, source_target_pairs={{8,0},{16,8},{24,16},{32,24},{40,32},{48,40},{56,48},{64,56},{72,6... | collective-permute-start | bytes 393224 | tf_op jit(solution)/shard_map/ppermute | solution.py:23
  118.4 19.9 %copy-start.6 = (bf16[2,16,16,256]{3,2,1,0:T(8,128)(2,1)S(1)}, bf16[2,16,16,256]{3,2,1,0:T(8,128)(2,1)}, u32[]{:S(2)}) copy-start(bf16[2,16,16,256]{3,2,1,0:T(8,128)(2,1)} %get-tuple-element.28) | copy-start | bytes 786436
  120.7 101.6 %copy-start.2 = (bf16[3,3,3,256,256]{3,4,2,1,0:T(8,128)(2,1)S(1)}, bf16[3,3,3,256,256]{3,4,2,1,0:T(8,128)(2,1)}, u32[]{:S(2)}) copy-start(bf16[3,3,3,256,256]{3,4,2,1,0:T(8,128)(2,1)} %rev.3) | copy-start | bytes 10616836
  146.0 3.5 %collective-permute-start.4 = (f32[216,256]{1,0:T(8,128)S(1)}, f32[216,256]{1,0:T(8,128)S(1)}, u32[]{:S(2)}, u32[]{:S(2)}) collective-permute-start(f32[216,256]{1,0:T(8,128)S(1)} %broadcast_multiply_fusion), channel_id=1, source_target_pairs={{0,1},{1,0},{2,3},{3,2},{4,5},{5,4},{6,7},{7,6},{8,9},{9,8},{10,11... | collective-permute-start | bytes 663560 | tf_op jit(solution)/shard_map/ppermute | solution.py:41
  149.6 0.7 copy-start.7
  154.6 18.0 %all-to-all-start = ((f32[32,1,3]{2,1,0:T(1,128)}), f32[32,1,3]{2,1,0:T(1,128)S(1)}, u32[]{:S(2)}, u32[]{:S(2)}) async-start(f32[32,1,3]{2,1,0:T(1,128)} %broadcast_in_dim.9), calls=%async_computation.2 | async-start | bytes 32768 | tf_op jit(solution)/shard_map/all_to_all | solution.py:46
  178.2 6.5 %copy-start.4 = (f32[216,256]{1,0:T(8,128)}, f32[216,256]{1,0:T(8,128)S(1)}, u32[]{:S(2)}) copy-start(f32[216,256]{1,0:T(8,128)S(1)} %multiply_add_fusion.1) | copy-start | bytes 663556
  178.3 6.5 %collective-permute-start.5 = (f32[216,256]{1,0:T(8,128)S(1)}, f32[216,256]{1,0:T(8,128)S(1)}, u32[]{:S(2)}, u32[]{:S(2)}) collective-permute-start(f32[216,256]{1,0:T(8,128)S(1)} %multiply_add_fusion.1), channel_id=1, source_target_pairs={{0,2},{2,0},{1,3},{3,1},{4,6},{6,4},{5,7},{7,5},{8,10},{10,8},{9,1... | collective-permute-start | bytes 663560 | tf_op jit(solution)/shard_map/ppermute | solution.py:41
  184.7 0.7 copy-start.8
  188.1 13.5 %all-to-all-start.1 = ((f32[32,1,3]{2,1,0:T(1,128)}), f32[32,1,3]{2,1,0:T(1,128)S(1)}, u32[]{:S(2)}, u32[]{:S(2)}) async-start(f32[32,1,3]{2,1,0:T(1,128)} %broadcast_in_dim.10), calls=%async_computation.3 | async-start | bytes 32768 | tf_op jit(solution)/shard_map/all_to_all | solution.py:46
  207.3 7.7 %copy-start.5 = (f32[216,256]{1,0:T(8,128)}, f32[216,256]{1,0:T(8,128)S(1)}, u32[]{:S(2)}) copy-start(f32[216,256]{1,0:T(8,128)S(1)} %multiply_add_fusion) | copy-start | bytes 663556
  207.3 7.7 %collective-permute-start.6 = (f32[216,256]{1,0:T(8,128)S(1)}, f32[216,256]{1,0:T(8,128)S(1)}, u32[]{:S(2)}, u32[]{:S(2)}) collective-permute-start(f32[216,256]{1,0:T(8,128)S(1)} %multiply_add_fusion), channel_id=1, source_target_pairs={{0,4},{4,0},{1,5},{5,1},{2,6},{6,2},{3,7},{7,3},{8,12},{12,8},{9,1... | collective-permute-start | bytes 663560 | tf_op jit(solution)/shard_map/ppermute | solution.py:41
  215.0 0.8 copy-start.10
  218.5 13.5 %all-to-all-start.2 = ((f32[32,1,3]{2,1,0:T(1,128)}), f32[32,1,3]{2,1,0:T(1,128)S(1)}, u32[]{:S(2)}, u32[]{:S(2)}) async-start(f32[32,1,3]{2,1,0:T(1,128)} %broadcast_in_dim.11), calls=%async_computation.4 | async-start | bytes 32768 | tf_op jit(solution)/shard_map/all_to_all | solution.py:46
Sparse Core Ops, SparseCore 0:
  30.9 87.4 reduce-scatter.2
  120.9 24.0 reduce-scatter.4
where the time goes:
time: 245 us; the launch traced here: 244 us
  waiting for transfers between devices  102 us (42%)
  local copies, waits for them, and re-layouts  56.5 us (23%)
  starting transfers between devices  29.2 us (12%)
  between operations  22.3 us (9%)
  other arithmetic  21.3 us (9%)
  matrix products  12.9 us (5%)
    reduce_scatter x2, waiting for transfers between devices, summed_rows(): x = lax.psum_scatter(x, axis, scatter_dimension=dim, tiled=True)  71.7 us
    unnamed x77, local copies, waits for them, and re-layouts  42.6 us
    all_to_all x3, waiting for transfers between devices, sent_to_all(): return lax.all_to_all(copies, axis, split_axis=0, concat_axis=0, tiled=True)  20 us
    all_to_all x3, starting transfers between devices, sent_to_all(): return lax.all_to_all(copies, axis, split_axis=0, concat_axis=0, tiled=True)  16 us
    ppermute x2, starting transfers between devices, with_halo(): before = lax.ppermute(last, axis, up)  7.45 us
    concatenate x3, other arithmetic, packed_total(): total = taken_together(jnp.concatenate([a.ravel() for a in arrays]), axis)  6.09 us
    dot_general x1, matrix products, shards(): jnp.dot(grad_columns, kernel_flip, preferred_element_type=jnp.float32)  5.7 us
    dot_general x1, matrix products, shards(): lax.dot_general(own_columns, pre_grad, contract, preferred_element_type=j...  5.17 us
  transfers between devices with their start and end apart: 12, of which 9 were waited for; matrix products, arithmetic and copies ran while one was open for 23% of the time, Pallas kernels for 0%

commit v1 on v0

v1 whole, which is shorter than its diff:
```python
import functools

import jax
import jax.numpy as jnp
from jax import lax
from jax.experimental import pallas as pl
from jax.experimental.pallas import tpu as pltpu
from jax.sharding import PartitionSpec as P

MESH = pl.DeviceIdType.MESH
EPS = 1e-06
F32, BF16 = jnp.float32, jnp.bfloat16
NX, NZ, NR = 4, 8, 8
FACTOR = 1.0 / 128.0

RIGHT = ((4, 0), (3, 1), (3, 0), (2, 1), (2, 0), (1, 1), (1, 0))
LEFT = ((4, 1), (3, 0), (3, 1), (2, 0), (2, 1), (1, 0), (1, 1))


def rcopy(src, dst, ss, rs, dev):
    return pltpu.make_async_remote_copy(
        src_ref=src, dst_ref=dst, send_sem=ss, recv_sem=rs, device_id=dev, device_id_type=MESH
    )


def adasum_weights(gram):
    groups = [[(v, None)] for v in range(NR)]
    dots = dict(gram)
    count = NR
    weights = [None] * NR
    members = [[v] for v in range(NR)]
    while count > 1:
        alpha = [None] * count
        for a in range(0, count, 2):
            b = a + 1
            half = 0.5 * dots[(a, b)]
            alpha[a] = 1.0 - half / (jnp.maximum(dots[(a, a)], 0.0) + EPS)
            alpha[b] = 1.0 - half / (jnp.maximum(dots[(b, b)], 0.0) + EPS)
        for a in range(count):
            for v in members[a]:
                weights[v] = alpha[a] if weights[v] is None else weights[v] * alpha[a]
        merged = {}
        half_count = count // 2
        for i in range(half_count):
            for j in range(i, half_count):
                total = None
                for a in (2 * i, 2 * i + 1):
                    for b in (2 * j, 2 * j + 1):
                        term = alpha[a] * alpha[b] * dots[(min(a, b), max(a, b))]
                        total = term if total is None else total + term
                merged[(i, j)] = total
        members = [members[2 * i] + members[2 * i + 1] for i in range(half_count)]
        dots = merged
        count = half_count
    return weights


def kernel(
    vol, cot, kern,
    gout, mout,
    x10, wk, cotv, ybuf, gbuf, gts, gtall, g3, acc, rsb, rfin, fsend, frecv, gr1, gr2, gr3, gsrc,
    lsem, xss, xrs, gss, grs, hss, hrs, rss, rrs, fss, frs, a1s, a1r, a2s, a2r, a3s, a3r,
):
    d = lax.axis_index("depth")
    rep = lax.axis_index("replica")
    z = d // NX
    x = lax.rem(d, NX)
    xr, xl = lax.rem(x + 1, NX), lax.rem(x + 3, NX)
    xo = lax.rem(x + 2, NX)
    zr, zl = lax.rem(z + 1, NZ), lax.rem(z + 7, NZ)

    bar = pltpu.get_barrier_semaphore()

    def greet(dd, rr):
        pl.semaphore_signal(bar, inc=1, device_id=(dd, rr), device_id_type=MESH)

    for dx in range(NX):
        for dr in range(NR):
            if dx or dr:
                greet(z * NX + lax.rem(x + dx, NX), lax.rem(rep + dr, NR))
    for dz in range(1, NZ):
        greet(lax.rem(z + dz, NZ) * NX + x, rep)

    @pl.when((x == 3) & (z < NZ - 1))
    def _():
        greet(d + 1, rep)

    @pl.when((x == 0) & (z > 0))
    def _():
        greet(d - 1, rep)

    rows = pl.ds(16, 256)
    lx = [pltpu.make_async_copy(vol.at[p], x10.at[1 + 2 * x + p, rows], lsem.at[p]) for p in range(2)]
    lw = pltpu.make_async_copy(kern, wk, lsem.at[2])
    lc = pltpu.make_async_copy(cot, cotv, lsem.at[3])
    for c in lx:
        c.start()
    lw.start()
    lc.start()
    pad = jnp.zeros((16, 256), BF16)
    for k in range(10):
        x10[k, 0:16, :] = pad
        x10[k, 272:288, :] = pad
    for k in range(4):
        gbuf[k, 0:16, :] = pad
        gbuf[k, 272:288, :] = pad

    @pl.when(z == 0)
    def _():
        x10[0, 16:272, :] = jnp.zeros((256, 256), BF16)

    @pl.when(z == NZ - 1)
    def _():
        x10[9, 16:272, :] = jnp.zeros((256, 256), BF16)

    @pl.when(d == 0)
    def _():
        gbuf[0, 16:272, :] = jnp.zeros((256, 256), BF16)

    @pl.when(d == NX * NZ - 1)
    def _():
        gbuf[3, 16:272, :] = jnp.zeros((256, 256), BF16)

    across = ((x == 3) & (z < NZ - 1)) | ((x == 0) & (z > 0))
    pl.semaphore_wait(bar, NX * NR - 1 + NZ - 1 + across.astype(jnp.int32))

    dr_, dl_ = z * NX + xr, z * NX + xl

    def plane(owner, p):
        return x10.at[1 + 2 * owner + p, rows]

    def to_right(p):
        return rcopy(vol.at[p], plane(x, p), xss.at[p], xrs.at[p], (dr_, rep))

    def to_left(p):
        return rcopy(vol.at[p], plane(x, p), xss.at[2 + p], xrs.at[2 + p], (dl_, rep))

    def from_left(p):
        return rcopy(vol.at[p], plane(xl, p), xss.at[p], xrs.at[p], (dr_, rep))

    def from_right(p):
        return rcopy(vol.at[p], plane(xr, p), xss.at[2 + p], xrs.at[2 + p], (dl_, rep))

    relay_r = rcopy(plane(xl, 0), plane(xl, 0), xss.at[4], xrs.at[4], (dr_, rep))
    relay_l = rcopy(plane(xr, 1), plane(xr, 1), xss.at[5], xrs.at[5], (dl_, rep))
    from_relay_l = rcopy(plane(xo, 0), plane(xo, 0), xss.at[4], xrs.at[4], (dr_, rep))
    from_relay_r = rcopy(plane(xo, 1), plane(xo, 1), xss.at[5], xrs.at[5], (dl_, rep))

    low, high = x10.at[0, rows], x10.at[9, rows]
    up_first = rcopy(vol.at[1], low, xss.at[6], xrs.at[6], (lax.rem(d + 1, NX * NZ), rep))
    down_first = rcopy(vol.at[0], high, xss.at[7], xrs.at[7], (lax.rem(d + NX * NZ - 1, NX * NZ), rep))
    up_last = rcopy(x10.at[8, rows], low, xss.at[8], xrs.at[6], (zr * NX + x, rep))
    down_last = rcopy(x10.at[1, rows], high, xss.at[9], xrs.at[7], (zl * NX + x, rep))

    @pl.when((x == 3) & (z < NZ - 1))
    def _():
        up_first.start()

    @pl.when((x == 0) & (z > 0))
    def _():
        down_first.start()

    to_right(1).start()
    to_left(0).start()
    to_right(0).start()
    to_left(1).start()

    for c in lx:
        c.wait()
    lw.wait()
    for p in range(2):
        taps = [(kd, kh) for kd in ((1, 2) if p == 0 else (0, 1)) for kh in range(3)]
        lhs = jnp.concatenate(
            [x10[2 * x + p + kd, kh * 16 : kh * 16 + 256, :] for kd, kh in taps], axis=1
        )
        for kw in range(3):
            rhs = jnp.concatenate([wk[kd * 3 + kh, kw] for kd, kh in taps], axis=0)
            ybuf[p, kw] = jnp.dot(lhs, rhs, preferred_element_type=F32)
    lc.wait()

    from_left(1).wait_recv()
    from_right(0).wait_recv()

    @pl.when((x == 0) & (z > 0))
    def _():
        up_first.wait_recv()

    @pl.when((x == 3) & (z < NZ - 1))
    def _():
        down_first.wait_recv()

    relay_l_ready = None
    w_of = lax.rem(lax.broadcasted_iota(jnp.int32, (256, 256), 0), 16)
    for p in range(2):
        kd = 0 if p == 0 else 2
        lhs = jnp.concatenate(
            [x10[2 * x + p + kd, kh * 16 : kh * 16 + 256, :] for kh in range(3)], axis=1
        )
        y = []
        for kw in range(3):
            rhs = jnp.concatenate([wk[kd * 3 + kh, kw] for kh in range(3)], axis=0)
            y.append(ybuf[p, kw] + jnp.dot(lhs, rhs, preferred_element_type=F32))
        preact = (
            y[1]
            + jnp.where(w_of >= 1, pltpu.roll(y[0], 1, 0), 0.0)
            + jnp.where(w_of <= 14, pltpu.roll(y[2], 255, 0), 0.0)
        )
        s = jax.nn.sigmoid(preact)
        g = (cotv[p].astype(F32) * s * (1.0 + preact * (1.0 - s))).astype(BF16)
        gbuf[1 + p, 16:272, :] = g
        gt = g.astype(F32).T.astype(BF16)
        for q in range(NX):
            gts[q, :, p * 256 : p * 256 + 256] = gt[q * 64 : q * 64 + 64, :]

    def g_send(dx):
        q = lax.rem(x + dx, NX)
        return rcopy(gts.at[q], gtall.at[x], gss.at[dx], grs.at[dx], (z * NX + q, rep))

    def g_recv(dx):
        q = lax.rem(x + NX - dx, NX)
        return rcopy(gts.at[q], gtall.at[q], gss.at[dx], grs.at[dx], (z * NX + q, rep))

    for dx in (2, 1, 3):
        g_send(dx).start()
    gtall[x] = gts[x]

    from_left(0).wait_recv()
    relay_r.start()
    from_right(1).wait_recv()
    relay_l.start()

    from_relay_l.wait_recv()
    from_relay_r.wait_recv()

    @pl.when((z < NZ - 1) & (x != 0))
    def _():
        up_last.start()

    @pl.when((z > 0) & (x != 3))
    def _():
        down_last.start()

    g_up = rcopy(gbuf.at[2, rows], gbuf.at[0, rows], hss.at[0], hrs.at[0], (lax.rem(d + 1, NX * NZ), rep))
    g_down = rcopy(
        gbuf.at[1, rows], gbuf.at[3, rows], hss.at[1], hrs.at[1], (lax.rem(d + NX * NZ - 1, NX * NZ), rep)
    )

    @pl.when(d < NX * NZ - 1)
    def _():
        g_up.start()

    @pl.when(d > 0)
    def _():
        g_down.start()

    for dx in (1, 3, 2):
        g_recv(dx).wait_recv()
    lane = lax.rem(lax.broadcasted_iota(jnp.int32, (64, 512), 1), 16)
    for q in range(NX):
        t = gtall[q].astype(F32)
        cols = slice(q * 512, q * 512 + 512)
        g3[0:64, cols] = jnp.where(lane <= 14, pltpu.roll(t, 511, 1), 0.0).astype(BF16)
        g3[64:128, cols] = t.astype(BF16)
        last = jnp.where(lane >= 1, pltpu.roll(t, 1, 1), 0.0).astype(BF16)
        g3[128:192, cols] = last
        g3[192:256, cols] = last

    @pl.when((z > 0) & (x != 0))
    def _():
        up_last.wait_recv()

    @pl.when((z < NZ - 1) & (x != 3))
    def _():
        down_last.wait_recv()

    for b in range(9):
        kd, kh = b // 3, b % 3
        field = x10[kd : kd + 8, kh * 16 : kh * 16 + 256, :].reshape(2048, 256)
        out = jnp.dot(g3[...], field, preferred_element_type=F32).T
        pair, twice = out[:, 0:128], out[:, 128:256]
        swapped = pltpu.roll(pair, 64, 1)
        for kw in range(3):
            start = (3 * b + kw) * 256
            at = start
            while at < start + 256:
                block = at // 216
                end = min(start + 256, (block + 1) * 216)
                k, q = block // 4, block % 4
                side, h = q // 2, q % 2
                source = twice if kw == 2 else (pair if kw == side else swapped)
                acc[k, h, at - block * 216 : end - block * 216, side * 64 : side * 64 + 64] = source[
                    at - start : end - start, side * 64 : side * 64 + 64
                ]
                at = end

    def unit(side, j):
        dist, h = (RIGHT, LEFT)[side][j]
        k = lax.rem(z + dist, NZ) if side == 0 else lax.rem(z + NZ - dist, NZ)
        there = zr if side == 0 else zl
        return rcopy(
            acc.at[k, h], rsb.at[side, j], rss.at[side, j], rrs.at[side, j], (there * NX + x, rep)
        )

    def send_unit(side, j):
        seq = (RIGHT, LEFT)[side]
        dist, h = seq[j]
        if (dist + 1, h) in seq:
            i = seq.index((dist + 1, h))
            k = lax.rem(z + dist, NZ) if side == 0 else lax.rem(z + NZ - dist, NZ)
            unit(side, i).wait_recv()
            acc[k, h] = acc[k, h] + rsb[side, i]
        unit(side, j).start()

    for j in range(2):
        for side in range(2):
            send_unit(side, j)

    @pl.when(d > 0)
    def _():
        g_up.wait_recv()

    @pl.when(d < NX * NZ - 1)
    def _():
        g_down.wait_recv()

    nt = (((1,), (1,)), ((), ()))

    def field_grad(p):
        lhs = jnp.concatenate(
            [
                gbuf[2 + p - kd, (2 - kh) * 16 : (2 - kh) * 16 + 256, :]
                for kd in range(3)
                for kh in range(3)
            ],
            axis=1,
        )
        y = []
        for kw in range(3):
            rhs = jnp.concatenate([wk[b, kw] for b in range(9)], axis=1)
            y.append(lax.dot_general(lhs, rhs, nt, preferred_element_type=F32))
        total = (
            y[1]
            + jnp.where(w_of <= 14, pltpu.roll(y[0], 255, 0), 0.0)
            + jnp.where(w_of >= 1, pltpu.roll(y[2], 1, 0), 0.0)
        )
        gout[p] = total.astype(BF16)

    field_grad(0)
    for side in range(2):
        send_unit(side, 2)
    field_grad(1)
    for j in range(3, 7):
        for side in range(2):
            send_unit(side, j)

    which = lax.broadcasted_iota(jnp.int32, (56, 128), 1) // 32
    for h in range(2):
        rfin[h, 216:224, :] = jnp.zeros((8, 128), F32)

    def owner_copy(q, j):
        return rcopy(
            fsend.at[2 * q + j], frecv.at[rep], fss.at[2 * q + j], frs.at[rep], (z * NX + q, 2 * x + j)
        )

    def owner_local(q, j):
        return pltpu.make_async_copy(fsend.at[2 * q + j], frecv.at[rep], fss.at[2 * q + j])

    for h in (1, 0):
        ir, il = RIGHT.index((1, h)), LEFT.index((1, h))
        unit(0, ir).wait_recv()
        unit(1, il).wait_recv()
        rfin[h, 0:216, :] = (acc[z, h] + rsb[0, ir] + rsb[1, il]) * FACTOR
        for side in range(2):
            q = 2 * side + h
            for j in range(2):
                packed = jnp.zeros((56, 128), F32)
                for m in range(4):
                    part = rfin[h, m * 56 : m * 56 + 56, :]
                    shift = (32 * (m - 2 * side - j)) % 128
                    if shift:
                        part = pltpu.roll(part, shift, 1)
                    packed = jnp.where(which == m, part, packed)
                fsend[2 * q + j] = packed
                here = (x == q) & (rep == 2 * x + j)

                @pl.when(here)
                def _():
                    owner_local(q, j).start()

                @pl.when(jnp.logical_not(here))
                def _():
                    owner_copy(q, j).start()

    for v in range(NR):
        mine = (x == rep // 2) & (rep == v)

        @pl.when(jnp.logical_not(mine))
        def _():
            rcopy(
                fsend.at[v], frecv.at[v], fss.at[v], frs.at[v], (d, lax.rem(rep + 1, NR))
            ).wait_recv()

    for q in range(NX):
        for j in range(2):
            here = (x == q) & (rep == 2 * x + j)

            @pl.when(here)
            def _():
                owner_local(q, j).wait()

            @pl.when(jnp.logical_not(here))
            def _():
                owner_copy(q, j).wait_send()

    lanes = lax.broadcasted_iota(jnp.int32, (8, 128), 1)
    pairs = [(u, v) for u in range(NR) for v in range(u, NR)]
    part = jnp.zeros((8, 128), F32)
    for n, (u, v) in enumerate(pairs):
        prod = frecv[u] * frecv[v]
        total = prod[0:8]
        for m in range(1, 7):
            total = total + prod[8 * m : 8 * m + 8]
        part = jnp.where(lanes == n, jnp.sum(total, axis=1, keepdims=True), part)

    def all_sum(value, index, count, buf, slot, ss, rs, dev):
        gsrc[slot] = value
        buf[index] = value

        def to(i):
            other = lax.rem(index + i, count)
            return rcopy(gsrc.at[slot], buf.at[index], ss.at[i], rs.at[i], dev(other))

        def back(i):
            other = lax.rem(index + count - i, count)
            return rcopy(gsrc.at[slot], buf.at[other], ss.at[i], rs.at[i], dev(other))

        for i in range(1, count):
            to(i).start()
        for i in range(1, count):
            back(i).wait_recv()
        for i in range(1, count):
            to(i).wait_send()
        total = buf[0]
        for i in range(1, count):
            total = total + buf[i]
        return total

    part = all_sum(part, rep, NR, gr1, 0, a1s, a1r, lambda o: (d, o))
    part = all_sum(part, x, NX, gr2, 1, a2s, a2r, lambda o: (z * NX + o, rep))
    part = all_sum(part, z, NZ, gr3, 2, a3s, a3r, lambda o: (o * NX + x, rep))
    whole = jnp.sum(part, axis=0, keepdims=True)
    row = lanes[0:1]
    gram = {
        uv: jnp.sum(jnp.where(row == n, whole, 0.0), axis=1, keepdims=True)
        for n, uv in enumerate(pairs)
    }
    weights = adasum_weights(gram)
    merged = weights[0] * frecv[0]
    for v in range(1, NR):
        merged = merged + weights[v] * frecv[v]
    for m in range(4):
        part = pltpu.roll(merged, 128 - 32 * m, 1) if m else merged
        count = min(56, 216 - 56 * m)
        mout[m * 56 : m * 56 + count, :] = part[0:count, 0:32]

    for p in range(2):
        to_right(p).wait_send()
        to_left(p).wait_send()
    relay_r.wait_send()
    relay_l.wait_send()

    @pl.when((x == 3) & (z < NZ - 1))
    def _():
        up_first.wait_send()

    @pl.when((x == 0) & (z > 0))
    def _():
        down_first.wait_send()

    @pl.when((z < NZ - 1) & (x != 0))
    def _():
        up_last.wait_send()

    @pl.when((z > 0) & (x != 3))
    def _():
        down_last.wait_send()

    for dx in range(1, NX):
        g_send(dx).wait_send()

    @pl.when(d < NX * NZ - 1)
    def _():
        g_up.wait_send()

    @pl.when(d > 0)
    def _():
        g_down.wait_send()

    for side in range(2):
        for j in range(7):
            unit(side, j).wait_send()


def shards(volume, cotangent, kernel_weights):
    dma = pltpu.SemaphoreType.DMA
    any_space = pl.BlockSpec(memory_space=pl.ANY)
    vmem = pl.BlockSpec(memory_space=pltpu.VMEM)
    gout, mout = pl.pallas_call(
        kernel,
        name="adasum_step",
        out_shape=(
            jax.ShapeDtypeStruct((2, 256, 256), BF16),
            jax.ShapeDtypeStruct((216, 32), F32),
        ),
        in_specs=[any_space] * 3,
        out_specs=(vmem, vmem),
        scratch_shapes=[
            pltpu.VMEM((10, 288, 256), BF16),
            pltpu.VMEM((9, 3, 256, 256), BF16),
            pltpu.VMEM((2, 256, 256), BF16),
            pltpu.VMEM((2, 3, 256, 256), F32),
            pltpu.VMEM((4, 288, 256), BF16),
            pltpu.VMEM((4, 64, 512), BF16),
            pltpu.VMEM((4, 64, 512), BF16),
            pltpu.VMEM((256, 2048), BF16),
            pltpu.VMEM((8, 2, 216, 128), F32),
            pltpu.VMEM((2, 7, 216, 128), F32),
            pltpu.VMEM((2, 224, 128), F32),
            pltpu.VMEM((8, 56, 128), F32),
            pltpu.VMEM((8, 56, 128), F32),
            pltpu.VMEM((8, 8, 128), F32),
            pltpu.VMEM((4, 8, 128), F32),
            pltpu.VMEM((8, 8, 128), F32),
            pltpu.VMEM((3, 8, 128), F32),
            dma((4,)),
            dma((10,)), dma((8,)),
            dma((4,)), dma((4,)),
            dma((2,)), dma((2,)),
            dma((2, 7)), dma((2, 7)),
            dma((8,)), dma((8,)),
            dma((8,)), dma((8,)),
            dma((4,)), dma((4,)),
            dma((8,)), dma((8,)),
        ],
        compiler_params=pltpu.CompilerParams(
            collective_id=0, has_side_effects=True, vmem_limit_bytes=56 * 1024 * 1024
        ),
    )(
        volume.reshape(2, 256, 256),
        cotangent.reshape(2, 256, 256),
        kernel_weights.reshape(9, 3, 256, 256),
    )
    return gout.reshape(1, 2, 16, 16, 256), mout


def solution(mesh):
    return jax.shard_map(
        shards,
        mesh=mesh,
        in_specs=(P("replica", "depth"), P("replica", "depth"), P()),
        out_specs=(P("replica", "depth"), P("depth", "replica")),
        check_vma=False,
    )
```

time: 245 us -> 75.7 us (0.31)
  waiting for transfers between devices: 102 us -> 0 us
  Pallas kernels: 0 us -> 71.4 us
  local copies, waits for them, and re-layouts: 56.5 us -> 3.26 us
  starting transfers between devices: 29.2 us -> 0 us
  between operations: 22.3 us -> 0.64 us
  other arithmetic: 21.3 us -> 0 us
  matrix products: 12.9 us -> 0 us
    reduce_scatter x2 -> x0, waiting for transfers between devices: 71.7 us -> none  [summed_rows(): x = lax.psum_scatter(x, axis, scatter_dimension=dim, tiled=True)]
    pallas_call x0 -> x1, Pallas kernels: none -> 71.4 us  [shards(): pl.pallas_call(kernel, name='adasum_step', out_shape=(jax.ShapeDtypeStruc...]
    unnamed x77 -> x2, local copies, waits for them, and re-layouts: 42.6 us -> 3.26 us
    all_to_all x3 -> x0, waiting for transfers between devices: 20 us -> none  [sent_to_all(): return lax.all_to_all(copies, axis, split_axis=0, concat_axis=0, tiled=True)]
    all_to_all x3 -> x0, starting transfers between devices: 16 us -> none  [sent_to_all(): return lax.all_to_all(copies, axis, split_axis=0, concat_axis=0, tiled=True)]
    ppermute x7 -> x0, starting transfers between devices: 13.1 us -> none  [the longest x2 7.45 us: with_halo(): before = lax.ppermute(last, axis, up)]
    dot_general x3 -> x0, matrix products: 12.9 us -> none  [the longest x1 5.7 us: shards(): jnp.dot(grad_columns, kernel_flip, preferred_element_type=jnp.float32)]
    concatenate x7 -> x0, other arithmetic: 10.8 us -> none  [the longest x3 6.09 us: packed_total(): total = taken_together(jnp.concatenate([a.ravel() for a in arrays]), axis)]
  transfers between devices with their start and end apart: 12 -> 0, of which waited for: 9 -> 0; matrix products, arithmetic and copies ran while one was open for 23% -> 0% of each run, Pallas kernels for 0% -> 0%
where the time goes in v1:
time: 75.7 us; the launch traced here: 75.3 us
  Pallas kernels  71.4 us (94%)
  local copies, waits for them, and re-layouts  3.26 us (4%)
    pallas_call x1, Pallas kernels, shards(): pl.pallas_call(kernel, name='adasum_step', out_shape=(jax.ShapeDtypeStruc...  71.4 us
    unnamed x2, local copies, waits for them, and re-layouts  3.26 us

profile of v1, /device:TPU:8, one launch (start us, length us, event | category | flops | bytes accessed | tf_op | source)
XLA Modules:
  0.0 75.3 jit_solution(15234496110399079347)
XLA Ops:
  0.6 71.4 %adasum_step.1 = (bf16[2,256,256]{2,1,0:T(8,128)(2,1)}, f32[216,32]{1,0:T(8,128)}) custom-call(bf16[2,256,256]{2,1,0:T(8,128)(2,1)} %bitcast.5, bf16[2,256,256]{2,1,0:T(8,128)(2,1)} %bitcast.6, bf16[9,3,256,256]{3,2,1,0:T(8,128)(2,1)} %bitcast.4), custom_call_target="tpu_custom_call" | custom-call | tf_op jit(solution)/shard_map/adasum_step/pallas_call | solution.py:508
  72.1 1.6 %copy.5 = f32[216,32]{0,1:T(8,128)} copy(f32[216,32]{1,0:T(8,128)} %get-tuple-element.7) | data formatting | bytes 55296
  73.7 1.7 %copy.7 = bf16[1,2,16,16,256]{4,3,2,1,0:T(8,128)(2,1)} copy(bf16[1,2,16,16,256]{4,3,2,1,0:T(8,128)(2,1)} %bitcast.7) | data formatting | bytes 524288

commit v2 on v1

--- a/solution.py
+++ b/solution.py
@@ -13,10 +13,6 @@
 NX, NZ, NR = 4, 8, 8
 FACTOR = 1.0 / 128.0
 
-RIGHT = ((4, 0), (3, 1), (3, 0), (2, 1), (2, 0), (1, 1), (1, 0))
-LEFT = ((4, 1), (3, 0), (3, 1), (2, 0), (2, 1), (1, 0), (1, 1))
-
-
 def rcopy(src, dst, ss, rs, dev):
     return pltpu.make_async_remote_copy(
         src_ref=src, dst_ref=dst, send_sem=ss, recv_sem=rs, device_id=dev, device_id_type=MESH
@@ -24,7 +20,6 @@
 
 
 def adasum_weights(gram):
-    groups = [[(v, None)] for v in range(NR)]
     dots = dict(gram)
     count = NR
     weights = [None] * NR
@@ -58,8 +53,8 @@
 def kernel(
     vol, cot, kern,
     gout, mout,
-    x10, wk, cotv, ybuf, gbuf, gts, gtall, g3, acc, rsb, rfin, fsend, frecv, gr1, gr2, gr3, gsrc,
-    lsem, xss, xrs, gss, grs, hss, hrs, rss, rrs, fss, frs, a1s, a1r, a2s, a2r, a3s, a3r,
+    x10, wk, cotv, ybuf, gbuf, gts, gtall, g3, acc, rsb, nsend, nrecv, rfin, fsend, frecv, gr1, gr2, gsrc,
+    lsem, rdy, xss, xrs, gss, grs, hss, hrs, rss, rrs, fss, frs, a1s, a1r, a2s, a2r,
 ):
     d = lax.axis_index("depth")
     rep = lax.axis_index("replica")
@@ -69,25 +64,52 @@
     xo = lax.rem(x + 2, NX)
     zr, zl = lax.rem(z + 1, NZ), lax.rem(z + 7, NZ)
 
+    sends, expected = [], {}
+
+    def go(copy, cond=None):
+        sends.append((copy, cond))
+        if cond is None:
+            copy.start()
+        else:
+            pl.when(cond)(copy.start)
+
+    def expect(key, copy, cond=None):
+        expected[key] = (copy, cond)
+
+    def got(key):
+        copy, cond = expected.pop(key)
+        if cond is None:
+            copy.wait_recv()
+        else:
+            pl.when(cond)(copy.wait_recv)
+
+    def finish():
+        for key in list(expected):
+            got(key)
+        for copy, cond in sends:
+            if cond is None:
+                copy.wait_send()
+            else:
+                pl.when(cond)(copy.wait_send)
+
     bar = pltpu.get_barrier_semaphore()
 
     def greet(dd, rr):
         pl.semaphore_signal(bar, inc=1, device_id=(dd, rr), device_id_type=MESH)
 
-    for dx in range(NX):
-        for dr in range(NR):
-            if dx or dr:
-                greet(z * NX + lax.rem(x + dx, NX), lax.rem(rep + dr, NR))
-    for dz in range(1, NZ):
-        greet(lax.rem(z + dz, NZ) * NX + x, rep)
-
-    @pl.when((x == 3) & (z < NZ - 1))
-    def _():
-        greet(d + 1, rep)
-
-    @pl.when((x == 0) & (z > 0))
-    def _():
-        greet(d - 1, rep)
+    core = lax.rem(rep, 2)
+    near = [
+        (d, rep + 1 - 2 * core),
+        (d, lax.rem(rep + 2, NR)),
+        (d, lax.rem(rep + 6, NR)),
+    ]
+    for dev in near + [(z * NX + xo, rep), (z * NX + xr, rep), (z * NX + xl, rep), (zr * NX + x, rep), (zl * NX + x, rep)]:
+        greet(*dev)
+
+    d_up, d_down = lax.rem(d + 1, NX * NZ), lax.rem(d + NX * NZ - 1, NX * NZ)
+    at_top, at_bottom = (x == 3) & (z < NZ - 1), (x == 0) & (z > 0)
+    pl.when(at_top)(lambda: greet(d_up, rep))
+    pl.when(at_bottom)(lambda: greet(d_down, rep))
 
     rows = pl.ds(16, 256)
     lx = [pltpu.make_async_copy(vol.at[p], x10.at[1 + 2 * x + p, rows], lsem.at[p]) for p in range(2)]
@@ -121,8 +143,7 @@
     def _():
         gbuf[3, 16:272, :] = jnp.zeros((256, 256), BF16)
 
-    across = ((x == 3) & (z < NZ - 1)) | ((x == 0) & (z > 0))
-    pl.semaphore_wait(bar, NX * NR - 1 + NZ - 1 + across.astype(jnp.int32))
+    pl.semaphore_wait(bar, 8 + (at_top | at_bottom).astype(jnp.int32))
 
     dr_, dl_ = z * NX + xr, z * NX + xl
 
@@ -141,32 +162,40 @@
     def from_right(p):
         return rcopy(vol.at[p], plane(xr, p), xss.at[2 + p], xrs.at[2 + p], (dl_, rep))
 
-    relay_r = rcopy(plane(xl, 0), plane(xl, 0), xss.at[4], xrs.at[4], (dr_, rep))
-    relay_l = rcopy(plane(xr, 1), plane(xr, 1), xss.at[5], xrs.at[5], (dl_, rep))
-    from_relay_l = rcopy(plane(xo, 0), plane(xo, 0), xss.at[4], xrs.at[4], (dr_, rep))
-    from_relay_r = rcopy(plane(xo, 1), plane(xo, 1), xss.at[5], xrs.at[5], (dl_, rep))
+    relay_r = rcopy(plane(xl, 1), plane(xl, 1), xss.at[4], xrs.at[4], (dr_, rep))
+    relay_l = rcopy(plane(xr, 0), plane(xr, 0), xss.at[5], xrs.at[5], (dl_, rep))
+    from_relay_l = rcopy(plane(xo, 1), plane(xo, 1), xss.at[4], xrs.at[4], (dr_, rep))
+    from_relay_r = rcopy(plane(xo, 0), plane(xo, 0), xss.at[5], xrs.at[5], (dl_, rep))
 
     low, high = x10.at[0, rows], x10.at[9, rows]
-    up_first = rcopy(vol.at[1], low, xss.at[6], xrs.at[6], (lax.rem(d + 1, NX * NZ), rep))
-    down_first = rcopy(vol.at[0], high, xss.at[7], xrs.at[7], (lax.rem(d + NX * NZ - 1, NX * NZ), rep))
-    up_last = rcopy(x10.at[8, rows], low, xss.at[8], xrs.at[6], (zr * NX + x, rep))
-    down_last = rcopy(x10.at[1, rows], high, xss.at[9], xrs.at[7], (zl * NX + x, rep))
-
-    @pl.when((x == 3) & (z < NZ - 1))
-    def _():
-        up_first.start()
-
-    @pl.when((x == 0) & (z > 0))
-    def _():
-        down_first.start()
-
-    to_right(1).start()
-    to_left(0).start()
-    to_right(0).start()
-    to_left(1).start()
-
+    up_first = rcopy(vol.at[1], low, xss.at[6], xrs.at[6], (d_up, rep))
+    down_first = rcopy(vol.at[0], high, xss.at[7], xrs.at[7], (d_down, rep))
+    up = rcopy(x10.at[8, rows], low, xss.at[8], xrs.at[6], (zr * NX + x, rep))
+    down = rcopy(x10.at[1, rows], high, xss.at[9], xrs.at[7], (zl * NX + x, rep))
+    is_low, is_high = z > 0, z < NZ - 1
+
+    go(up_first, at_top)
+    go(down_first, at_bottom)
+    go(to_right(1))
+    go(to_left(0))
+    go(to_right(0))
+    go(to_left(1))
+    for dev in ((zr * NX + x, rep), (zl * NX + x, rep)):
+        pl.semaphore_signal(rdy.at[3], inc=1, device_id=dev, device_id_type=MESH)
     for c in lx:
         c.wait()
+    go(up, is_high & (x == 3))
+    go(down, is_low & (x == 0))
+    for p in range(2):
+        expect(("left", p), from_left(p))
+        expect(("right", p), from_right(p))
+    expect("low0", up, at_bottom)
+    expect("high0", down, at_top)
+    expect("low1", up, is_low & (x != 0))
+    expect("high1", down, is_high & (x != 3))
+    expect("relay_l", from_relay_l)
+    expect("relay_r", from_relay_r)
+
     lw.wait()
     for p in range(2):
         taps = [(kd, kh) for kd in ((1, 2) if p == 0 else (0, 1)) for kh in range(3)]
@@ -178,18 +207,12 @@
             ybuf[p, kw] = jnp.dot(lhs, rhs, preferred_element_type=F32)
     lc.wait()
 
-    from_left(1).wait_recv()
-    from_right(0).wait_recv()
-
-    @pl.when((x == 0) & (z > 0))
-    def _():
-        up_first.wait_recv()
-
-    @pl.when((x == 3) & (z < NZ - 1))
-    def _():
-        down_first.wait_recv()
-
-    relay_l_ready = None
+    got(("left", 1))
+    go(relay_r)
+    got(("right", 0))
+    go(relay_l)
+    got("low0")
+    got("high0")
     w_of = lax.rem(lax.broadcasted_iota(jnp.int32, (256, 256), 0), 16)
     for p in range(2):
         kd = 0 if p == 0 else 2
@@ -221,40 +244,29 @@
         return rcopy(gts.at[q], gtall.at[q], gss.at[dx], grs.at[dx], (z * NX + q, rep))
 
     for dx in (2, 1, 3):
-        g_send(dx).start()
+        go(g_send(dx))
+        expect(("g", dx), g_recv(dx))
     gtall[x] = gts[x]
 
-    from_left(0).wait_recv()
-    relay_r.start()
-    from_right(1).wait_recv()
-    relay_l.start()
-
-    from_relay_l.wait_recv()
-    from_relay_r.wait_recv()
-
-    @pl.when((z < NZ - 1) & (x != 0))
-    def _():
-        up_last.start()
-
-    @pl.when((z > 0) & (x != 3))
-    def _():
-        down_last.start()
-
-    g_up = rcopy(gbuf.at[2, rows], gbuf.at[0, rows], hss.at[0], hrs.at[0], (lax.rem(d + 1, NX * NZ), rep))
+    got(("left", 0))
+    got(("right", 1))
+    got("relay_l")
+    got("relay_r")
+    inner = (x == 1) | (x == 2)
+    go(up, is_high & inner)
+    go(down, is_low & inner)
+
+    g_up = rcopy(gbuf.at[2, rows], gbuf.at[0, rows], hss.at[0], hrs.at[0], (d_up, rep))
     g_down = rcopy(
         gbuf.at[1, rows], gbuf.at[3, rows], hss.at[1], hrs.at[1], (lax.rem(d + NX * NZ - 1, NX * NZ), rep)
     )
-
-    @pl.when(d < NX * NZ - 1)
-    def _():
-        g_up.start()
-
-    @pl.when(d > 0)
-    def _():
-        g_down.start()
-
-    for dx in (1, 3, 2):
-        g_recv(dx).wait_recv()
+    go(g_up, d < NX * NZ - 1)
+    go(g_down, d > 0)
+    expect("g_low", g_up, d > 0)
+    expect("g_high", g_down, d < NX * NZ - 1)
+
+    for key in (("g", 1), ("g", 3), ("g", 2)):
+        got(key)
     lane = lax.rem(lax.broadcasted_iota(jnp.int32, (64, 512), 1), 16)
     for q in range(NX):
         t = gtall[q].astype(F32)
@@ -265,15 +277,11 @@
         g3[128:192, cols] = last
         g3[192:256, cols] = last
 
-    @pl.when((z > 0) & (x != 0))
-    def _():
-        up_last.wait_recv()
-
-    @pl.when((z < NZ - 1) & (x != 3))
-    def _():
-        down_last.wait_recv()
-
-    for b in range(9):
+
+    for b in (3, 4, 5, 0, 1, 2, 6, 7, 8):
+        if b == 0:
+            got("low1")
+            got("high1")
         kd, kh = b // 3, b % 3
         field = x10[kd : kd + 8, kh * 16 : kh * 16 + 256, :].reshape(2048, 256)
         out = jnp.dot(g3[...], field, preferred_element_type=F32).T
@@ -293,36 +301,56 @@
                 ]
                 at = end
 
-    def unit(side, j):
-        dist, h = (RIGHT, LEFT)[side][j]
-        k = lax.rem(z + dist, NZ) if side == 0 else lax.rem(z + NZ - dist, NZ)
-        there = zr if side == 0 else zl
-        return rcopy(
-            acc.at[k, h], rsb.at[side, j], rss.at[side, j], rrs.at[side, j], (there * NX + x, rep)
-        )
-
-    def send_unit(side, j):
-        seq = (RIGHT, LEFT)[side]
-        dist, h = seq[j]
-        if (dist + 1, h) in seq:
-            i = seq.index((dist + 1, h))
-            k = lax.rem(z + dist, NZ) if side == 0 else lax.rem(z + NZ - dist, NZ)
-            unit(side, i).wait_recv()
-            acc[k, h] = acc[k, h] + rsb[side, i]
-        unit(side, j).start()
-
-    for j in range(2):
+    def ready(t):
+        for dev in near:
+            pl.semaphore_signal(rdy.at[t], inc=1, device_id=dev, device_id_type=MESH)
+
+    half_of = (0, 1)
+
+    def far(side, dist):
+        return lax.rem(z + dist, NZ) if side == 0 else lax.rem(z + NZ - dist, NZ)
+
+    hops = {"a": (4, 2), "b": (3, 1), "c": (1, 1), "d": (2, 2)}
+
+    def unit(side, kind, h):
+        dist, step = hops[kind]
+        there = far(side, step) * NX + x
+        if kind == "d":
+            src, dst, n = acc.at[far(side, 2), h], rsb.at[side, h], 6 + h
+        else:
+            n = "abc".index(kind) * 2 + h
+            src, dst = nsend.at[side, n], nrecv.at[side, n]
+        return rcopy(src, dst, rss.at[side, n], rrs.at[side, n], (there, rep))
+
+    def send_unit(side, kind, h):
+        dist, _ = hops[kind]
+        k = far(side, dist)
+        if kind == "d":
+            got(("rs", side, "b", h))
+            value = acc[k, h] + nrecv[side, 2 + h].astype(F32)
+            if h == half_of[side]:
+                got(("rs", side, "a", h))
+                value = value + nrecv[side, h].astype(F32)
+            acc[k, h] = value
+        else:
+            nsend[side, "abc".index(kind) * 2 + h] = acc[k, h].astype(BF16)
+        go(unit(side, kind, h))
+        expect(("rs", side, kind, h), unit(side, kind, h))
+
+    pl.semaphore_wait(rdy.at[3], 2)
+    ready(0)
+    for side in range(2):
+        send_unit(side, "b", 1 - half_of[side])
+    for side in range(2):
+        send_unit(side, "a", half_of[side])
+    for side in range(2):
+        send_unit(side, "b", half_of[side])
+    for h in range(2):
         for side in range(2):
-            send_unit(side, j)
-
-    @pl.when(d > 0)
-    def _():
-        g_up.wait_recv()
-
-    @pl.when(d < NX * NZ - 1)
-    def _():
-        g_down.wait_recv()
-
+            send_unit(side, "c", h)
+
+    got("g_low")
+    got("g_high")
     nt = (((1,), (1,)), ((), ()))
 
     def field_grad(p):
@@ -345,13 +373,17 @@
         )
         gout[p] = total.astype(BF16)
 
+    pl.semaphore_wait(rdy.at[0], 3)
+    ready(1)
     field_grad(0)
     for side in range(2):
-        send_unit(side, 2)
+        send_unit(side, "d", 1 - half_of[side])
+    for side in range(2):
+        send_unit(side, "d", half_of[side])
+    pl.semaphore_wait(rdy.at[1], 3)
+    ready(2)
     field_grad(1)
-    for j in range(3, 7):
-        for side in range(2):
-            send_unit(side, j)
+    pl.semaphore_wait(rdy.at[2], 3)
 
     which = lax.broadcasted_iota(jnp.int32, (56, 128), 1) // 32
     for h in range(2):
@@ -366,10 +398,14 @@
         return pltpu.make_async_copy(fsend.at[2 * q + j], frecv.at[rep], fss.at[2 * q + j])
 
     for h in (1, 0):
-        ir, il = RIGHT.index((1, h)), LEFT.index((1, h))
-        unit(0, ir).wait_recv()
-        unit(1, il).wait_recv()
-        rfin[h, 0:216, :] = (acc[z, h] + rsb[0, ir] + rsb[1, il]) * FACTOR
+        total = acc[z, h]
+        for side in range(2):
+            got(("rs", side, "c", h))
+            total = total + nrecv[side, 4 + h].astype(F32)
+        for side in range(2):
+            got(("rs", side, "d", h))
+            total = total + rsb[side, h]
+        rfin[h, 0:216, :] = total * FACTOR
         for side in range(2):
             q = 2 * side + h
             for j in range(2):
@@ -383,34 +419,18 @@
                 fsend[2 * q + j] = packed
                 here = (x == q) & (rep == 2 * x + j)
 
-                @pl.when(here)
-                def _():
-                    owner_local(q, j).start()
-
-                @pl.when(jnp.logical_not(here))
-                def _():
-                    owner_copy(q, j).start()
+                pl.when(here)(owner_local(q, j).start)
+                go(owner_copy(q, j), jnp.logical_not(here))
 
     for v in range(NR):
         mine = (x == rep // 2) & (rep == v)
-
-        @pl.when(jnp.logical_not(mine))
-        def _():
-            rcopy(
-                fsend.at[v], frecv.at[v], fss.at[v], frs.at[v], (d, lax.rem(rep + 1, NR))
-            ).wait_recv()
-
+        copy = rcopy(fsend.at[v], frecv.at[v], fss.at[v], frs.at[v], (d, lax.rem(rep + 1, NR)))
+        expect(("own", v), copy, jnp.logical_not(mine))
     for q in range(NX):
         for j in range(2):
-            here = (x == q) & (rep == 2 * x + j)
-
-            @pl.when(here)
-            def _():
-                owner_local(q, j).wait()
-
-            @pl.when(jnp.logical_not(here))
-            def _():
-                owner_copy(q, j).wait_send()
+            pl.when((x == q) & (rep == 2 * x + j))(owner_local(q, j).wait)
+    for v in range(NR):
+        got(("own", v))
 
     lanes = lax.broadcasted_iota(jnp.int32, (8, 128), 1)
     pairs = [(u, v) for u in range(NR) for v in range(u, NR)]
@@ -435,20 +455,22 @@
             return rcopy(gsrc.at[slot], buf.at[other], ss.at[i], rs.at[i], dev(other))
 
         for i in range(1, count):
-            to(i).start()
+            go(to(i))
         for i in range(1, count):
             back(i).wait_recv()
-        for i in range(1, count):
-            to(i).wait_send()
         total = buf[0]
         for i in range(1, count):
             total = total + buf[i]
         return total
 
-    part = all_sum(part, rep, NR, gr1, 0, a1s, a1r, lambda o: (d, o))
-    part = all_sum(part, x, NX, gr2, 1, a2s, a2r, lambda o: (z * NX + o, rep))
-    part = all_sum(part, z, NZ, gr3, 2, a3s, a3r, lambda o: (o * NX + x, rep))
-    whole = jnp.sum(part, axis=0, keepdims=True)
+    part = jnp.sum(part, axis=0, keepdims=True)
+
+    def plane_dev(o):
+        return z * NX + o // NR, lax.rem(o, NR)
+
+    part = all_sum(part, x * NR + rep, NX * NR, gr1, 0, a1s, a1r, plane_dev)
+    part = all_sum(part, z, NZ, gr2, 1, a2s, a2r, lambda o: (o * NX + x, rep))
+    whole = part
     row = lanes[0:1]
     gram = {
         uv: jnp.sum(jnp.where(row == n, whole, 0.0), axis=1, keepdims=True)
@@ -458,47 +480,17 @@
     merged = weights[0] * frecv[0]
     for v in range(1, NR):
         merged = merged + weights[v] * frecv[v]
+    turned = merged.T
     for m in range(4):
-        part = pltpu.roll(merged, 128 - 32 * m, 1) if m else merged
         count = min(56, 216 - 56 * m)
-        mout[m * 56 : m * 56 + count, :] = part[0:count, 0:32]
-
-    for p in range(2):
-        to_right(p).wait_send()
-        to_left(p).wait_send()
-    relay_r.wait_send()
-    relay_l.wait_send()
-
-    @pl.when((x == 3) & (z < NZ - 1))
-    def _():
-        up_first.wait_send()
-
-    @pl.when((x == 0) & (z > 0))
-    def _():
-        down_first.wait_send()
-
-    @pl.when((z < NZ - 1) & (x != 0))
-    def _():
-        up_last.wait_send()
-
-    @pl.when((z > 0) & (x != 3))
-    def _():
-        down_last.wait_send()
-
-    for dx in range(1, NX):
-        g_send(dx).wait_send()
-
-    @pl.when(d < NX * NZ - 1)
-    def _():
-        g_up.wait_send()
-
-    @pl.when(d > 0)
-    def _():
-        g_down.wait_send()
-
-    for side in range(2):
-        for j in range(7):
-            unit(side, j).wait_send()
+        mout[:, m * 56 : m * 56 + count] = turned[m * 32 : m * 32 + 32, 0:count]
+
+    finish()
+
+
+def hand_over(g, m, g_out, m_out):
+    g_out[...] = g[...]
+    m_out[...] = m[...]
 
 
 def shards(volume, cotangent, kernel_weights):
@@ -510,7 +502,7 @@
         name="adasum_step",
         out_shape=(
             jax.ShapeDtypeStruct((2, 256, 256), BF16),
-            jax.ShapeDtypeStruct((216, 32), F32),
+            jax.ShapeDtypeStruct((32, 216), F32),
         ),
         in_specs=[any_space] * 3,
         out_specs=(vmem, vmem),
@@ -524,22 +516,23 @@
             pltpu.VMEM((4, 64, 512), BF16),
             pltpu.VMEM((256, 2048), BF16),
             pltpu.VMEM((8, 2, 216, 128), F32),
-            pltpu.VMEM((2, 7, 216, 128), F32),
+            pltpu.VMEM((2, 2, 216, 128), F32),
+            pltpu.VMEM((2, 6, 216, 128), BF16),
+            pltpu.VMEM((2, 6, 216, 128), BF16),
             pltpu.VMEM((2, 224, 128), F32),
             pltpu.VMEM((8, 56, 128), F32),
             pltpu.VMEM((8, 56, 128), F32),
-            pltpu.VMEM((8, 8, 128), F32),
-            pltpu.VMEM((4, 8, 128), F32),
-            pltpu.VMEM((8, 8, 128), F32),
-            pltpu.VMEM((3, 8, 128), F32),
+            pltpu.VMEM((32, 1, 128), F32),
+            pltpu.VMEM((8, 1, 128), F32),
+            pltpu.VMEM((2, 1, 128), F32),
             dma((4,)),
+            pltpu.SemaphoreType.REGULAR((4,)),
             dma((10,)), dma((8,)),
             dma((4,)), dma((4,)),
             dma((2,)), dma((2,)),
-            dma((2, 7)), dma((2, 7)),
+            dma((2, 8)), dma((2, 8)),
             dma((8,)), dma((8,)),
-            dma((8,)), dma((8,)),
-            dma((4,)), dma((4,)),
+            dma((32,)), dma((32,)),
             dma((8,)), dma((8,)),
         ],
         compiler_params=pltpu.CompilerParams(
@@ -550,7 +543,17 @@
         cotangent.reshape(2, 256, 256),
         kernel_weights.reshape(9, 3, 256, 256),
     )
-    return gout.reshape(1, 2, 16, 16, 256), mout
+    gout, mout = pl.pallas_call(
+        hand_over,
+        name="hand_over",
+        out_shape=(
+            jax.ShapeDtypeStruct((2, 256, 256), BF16),
+            jax.ShapeDtypeStruct((32, 216), F32),
+        ),
+        in_specs=[vmem] * 2,
+        out_specs=(vmem, vmem),
+    )(gout, mout)
+    return gout.reshape(1, 2, 16, 16, 256), mout.T
 
 
 def solution(mesh):

time: 75.7 us -> 65.8 us (0.87)
  Pallas kernels: 71.4 us -> 65 us
  local copies, waits for them, and re-layouts: 3.26 us -> 0 us
    pallas_call x1, Pallas kernels: 71.4 us -> 63.3 us  [shards(): pl.pallas_call(kernel, name='adasum_step', out_shape=(jax.ShapeDtypeStruc...]
    unnamed x2 -> x0, local copies, waits for them, and re-layouts: 3.26 us -> none
    pallas_call x0 -> x1, Pallas kernels: none -> 1.68 us  [shards(): pl.pallas_call(hand_over, name='hand_over', out_shape=(jax.ShapeDtypeStru...]
where the time goes in v2:
time: 65.8 us; the launch traced here: 65.6 us
  Pallas kernels  65 us (99%)
    pallas_call x1, Pallas kernels, shards(): pl.pallas_call(kernel, name='adasum_step', out_shape=(jax.ShapeDtypeStruc...  63.3 us
    pallas_call x1, Pallas kernels, shards(): pl.pallas_call(hand_over, name='hand_over', out_shape=(jax.ShapeDtypeStru...  1.68 us

profile of v2, /device:TPU:8, one launch (start us, length us, event | category | flops | bytes accessed | tf_op | source)
XLA Modules:
  0.0 65.6 jit_solution(12393192548973942731)
XLA Ops:
  0.6 63.3 %adasum_step.1 = (bf16[2,256,256]{2,1,0:T(8,128)(2,1)}, f32[32,216]{1,0:T(8,128)}) custom-call(bf16[2,256,256]{2,1,0:T(8,128)(2,1)} %bitcast.6, bf16[2,256,256]{2,1,0:T(8,128)(2,1)} %bitcast.7, bf16[9,3,256,256]{3,2,1,0:T(8,128)(2,1)} %bitcast.5), custom_call_target="tpu_custom_call" | custom-call | tf_op jit(solution)/shard_map/adasum_step/pallas_call | solution.py:500
  63.9 1.7 %hand_over.1 = (bf16[2,256,256]{2,1,0:T(8,128)(2,1)}, f32[32,216]{1,0:T(8,128)}) custom-call(bf16[2,256,256]{2,1,0:T(8,128)(2,1)} %get-tuple-element.6.g, f32[32,216]{1,0:T(8,128)} %get-tuple-element.7.m), custom_call_target="tpu_custom_call" | custom-call | tf_op jit(solution)/shard_map/hand_over/pallas_call | solution.py:546

commit v3 on v2

--- a/solution.py
+++ b/solution.py
@@ -340,14 +340,11 @@
     pl.semaphore_wait(rdy.at[3], 2)
     ready(0)
     for side in range(2):
-        send_unit(side, "b", 1 - half_of[side])
-    for side in range(2):
         send_unit(side, "a", half_of[side])
-    for side in range(2):
-        send_unit(side, "b", half_of[side])
-    for h in range(2):
-        for side in range(2):
-            send_unit(side, "c", h)
+    for kind in ("b", "c"):
+        for h in (1, 0):
+            for side in range(2):
+                send_unit(side, kind, h)
 
     got("g_low")
     got("g_high")
@@ -377,9 +374,9 @@
     ready(1)
     field_grad(0)
     for side in range(2):
-        send_unit(side, "d", 1 - half_of[side])
+        send_unit(side, "d", 1)
     for side in range(2):
-        send_unit(side, "d", half_of[side])
+        send_unit(side, "d", 0)
     pl.semaphore_wait(rdy.at[1], 3)
     ready(2)
     field_grad(1)
@@ -442,34 +439,31 @@
             total = total + prod[8 * m : 8 * m + 8]
         part = jnp.where(lanes == n, jnp.sum(total, axis=1, keepdims=True), part)
 
-    def all_sum(value, index, count, buf, slot, ss, rs, dev):
-        gsrc[slot] = value
-        buf[index] = value
-
-        def to(i):
-            other = lax.rem(index + i, count)
-            return rcopy(gsrc.at[slot], buf.at[index], ss.at[i], rs.at[i], dev(other))
-
-        def back(i):
-            other = lax.rem(index + count - i, count)
-            return rcopy(gsrc.at[slot], buf.at[other], ss.at[i], rs.at[i], dev(other))
-
-        for i in range(1, count):
-            go(to(i))
-        for i in range(1, count):
-            back(i).wait_recv()
-        total = buf[0]
-        for i in range(1, count):
-            total = total + buf[i]
-        return total
-
     part = jnp.sum(part, axis=0, keepdims=True)
 
-    def plane_dev(o):
-        return z * NX + o // NR, lax.rem(o, NR)
-
-    part = all_sum(part, x * NR + rep, NX * NR, gr1, 0, a1s, a1r, plane_dev)
-    part = all_sum(part, z, NZ, gr2, 1, a2s, a2r, lambda o: (o * NX + x, rep))
+    gsrc[0] = part
+    partner = rcopy(gsrc.at[0], gr1.at[0], a1s.at[0], a1r.at[0], near[0])
+    go(partner)
+    expect("partner", partner)
+    got("partner")
+    part = part + gr1[0]
+    gsrc[1] = part
+    chips = NX * NZ * NR // 2
+    chip = d * (NR // 2) + rep // 2
+    gr2[chip] = part
+
+    def tell(i, _):
+        other = lax.rem(chip + i, chips)
+        dev = (other // (NR // 2), lax.rem(other, NR // 2) * 2 + core)
+        rcopy(gsrc.at[1], gr2.at[chip], a2s.at[0], a2r.at[0], dev).start()
+        return 0
+
+    lax.fori_loop(1, chips, tell, 0)
+    rest = gr2.at[pl.ds(0, chips - 1)]
+    told = rcopy(rest, rest, a2s.at[0], a2r.at[0], near[0])
+    told.wait_recv()
+    told.wait_send()
+    part = jnp.sum(gr2[...], axis=0)
     whole = part
     row = lanes[0:1]
     gram = {
@@ -488,11 +482,6 @@
     finish()
 
 
-def hand_over(g, m, g_out, m_out):
-    g_out[...] = g[...]
-    m_out[...] = m[...]
-
-
 def shards(volume, cotangent, kernel_weights):
     dma = pltpu.SemaphoreType.DMA
     any_space = pl.BlockSpec(memory_space=pl.ANY)
@@ -501,8 +490,8 @@
         kernel,
         name="adasum_step",
         out_shape=(
-            jax.ShapeDtypeStruct((2, 256, 256), BF16),
-            jax.ShapeDtypeStruct((32, 216), F32),
+            pltpu.VMEM((2, 256, 256), BF16),
+            pltpu.VMEM((32, 216), F32),
         ),
         in_specs=[any_space] * 3,
         out_specs=(vmem, vmem),
@@ -522,8 +511,8 @@
             pltpu.VMEM((2, 224, 128), F32),
             pltpu.VMEM((8, 56, 128), F32),
             pltpu.VMEM((8, 56, 128), F32),
-            pltpu.VMEM((32, 1, 128), F32),
-            pltpu.VMEM((8, 1, 128), F32),
+            pltpu.VMEM((1, 1, 128), F32),
+            pltpu.VMEM((128, 1, 128), F32),
             pltpu.VMEM((2, 1, 128), F32),
             dma((4,)),
             pltpu.SemaphoreType.REGULAR((4,)),
@@ -532,8 +521,8 @@
             dma((2,)), dma((2,)),
             dma((2, 8)), dma((2, 8)),
             dma((8,)), dma((8,)),
-            dma((32,)), dma((32,)),
-            dma((8,)), dma((8,)),
+            dma((1,)), dma((1,)),
+            dma((1,)), dma((1,)),
         ],
         compiler_params=pltpu.CompilerParams(
             collective_id=0, has_side_effects=True, vmem_limit_bytes=56 * 1024 * 1024
@@ -543,16 +532,6 @@
         cotangent.reshape(2, 256, 256),
         kernel_weights.reshape(9, 3, 256, 256),
     )
-    gout, mout = pl.pallas_call(
-        hand_over,
-        name="hand_over",
-        out_shape=(
-            jax.ShapeDtypeStruct((2, 256, 256), BF16),
-            jax.ShapeDtypeStruct((32, 216), F32),
-        ),
-        in_specs=[vmem] * 2,
-        out_specs=(vmem, vmem),
-    )(gout, mout)
     return gout.reshape(1, 2, 16, 16, 256), mout.T
 
 

time: 65.8 us -> 63.8 us (0.970); the launches traced: 65.6 us -> 62.8 us
  Pallas kernels: 65 us -> 60.8 us
  local copies, waits for them, and re-layouts: 0 us -> 1.32 us
    pallas_call x2 -> x1, Pallas kernels: 65 us -> 60.8 us  [shards(): pl.pallas_call(kernel, name='adasum_step', out_shape=(pltpu.VMEM((2, 256,...]
    unnamed x0 -> x2, local copies, waits for them, and re-layouts: none -> 1.32 us
where the time goes in v3:
time: 63.8 us; the launch traced here: 62.8 us
  Pallas kernels  60.8 us (95%)
  local copies, waits for them, and re-layouts  1.32 us (2%)
  between operations  0.64 us (1%)
    pallas_call x1, Pallas kernels, shards(): pl.pallas_call(kernel, name='adasum_step', out_shape=(pltpu.VMEM((2, 256,...  60.8 us
    unnamed x2, local copies, waits for them, and re-layouts  1.32 us

profile of v3, /device:TPU:8, one launch (start us, length us, event | category | flops | bytes accessed | tf_op | source)
XLA Modules:
  0.0 62.8 jit_solution(2732942853473880404)
XLA Ops:
  0.6 60.8 %adasum_step.1 = (bf16[2,256,256]{2,1,0:T(8,128)(2,1)S(1)}, f32[32,216]{1,0:T(8,128)S(1)}) custom-call(bf16[2,256,256]{2,1,0:T(8,128)(2,1)} %bitcast.8, bf16[2,256,256]{2,1,0:T(8,128)(2,1)} %bitcast.9, bf16[9,3,256,256]{3,2,1,0:T(8,128)(2,1)} %bitcast.7), custom_call_target="tpu_custom_call" | custom-call | tf_op jit(solution)/shard_map/adasum_step/pallas_call | solution.py:489
  61.5 0.7 %copy.7 = bf16[1,2,16,16,256]{4,3,2,1,0:T(8,128)(2,1)} copy(bf16[1,2,16,16,256]{4,3,2,1,0:T(8,128)(2,1)S(1)} %bitcast.5) | data formatting | bytes 524288
  62.2 0.6 copy.8

commit v4 on v3

--- a/solution.py
+++ b/solution.py
@@ -255,6 +255,9 @@
     inner = (x == 1) | (x == 2)
     go(up, is_high & inner)
     go(down, is_low & inner)
+    pl.semaphore_wait(rdy.at[3], 2)
+    for dev in ((zr * NX + x, rep), (zl * NX + x, rep)):
+        pl.semaphore_signal(rdy.at[4], inc=1, device_id=dev, device_id_type=MESH)
 
     g_up = rcopy(gbuf.at[2, rows], gbuf.at[0, rows], hss.at[0], hrs.at[0], (d_up, rep))
     g_down = rcopy(
@@ -273,9 +276,7 @@
         cols = slice(q * 512, q * 512 + 512)
         g3[0:64, cols] = jnp.where(lane <= 14, pltpu.roll(t, 511, 1), 0.0).astype(BF16)
         g3[64:128, cols] = t.astype(BF16)
-        last = jnp.where(lane >= 1, pltpu.roll(t, 1, 1), 0.0).astype(BF16)
-        g3[128:192, cols] = last
-        g3[192:256, cols] = last
+        g3[128:192, cols] = jnp.where(lane >= 1, pltpu.roll(t, 1, 1), 0.0).astype(BF16)
 
 
     for b in (3, 4, 5, 0, 1, 2, 6, 7, 8):
@@ -284,7 +285,8 @@
             got("high1")
         kd, kh = b // 3, b % 3
         field = x10[kd : kd + 8, kh * 16 : kh * 16 + 256, :].reshape(2048, 256)
-        out = jnp.dot(g3[...], field, preferred_element_type=F32).T
+        out = jnp.dot(g3[...], field, preferred_element_type=F32)
+        out = jnp.concatenate([out, out[128:192]], axis=0).T
         pair, twice = out[:, 0:128], out[:, 128:256]
         swapped = pltpu.roll(pair, 64, 1)
         for kw in range(3):
@@ -310,13 +312,13 @@
     def far(side, dist):
         return lax.rem(z + dist, NZ) if side == 0 else lax.rem(z + NZ - dist, NZ)
 
-    hops = {"a": (4, 2), "b": (3, 1), "c": (1, 1), "d": (2, 2)}
+    hops = {"a": (4, 3), "b": (3, 2), "c": (2, 1), "d": (1, 1)}
 
     def unit(side, kind, h):
         dist, step = hops[kind]
         there = far(side, step) * NX + x
         if kind == "d":
-            src, dst, n = acc.at[far(side, 2), h], rsb.at[side, h], 6 + h
+            src, dst, n = acc.at[far(side, 1), h], rsb.at[side, h], 6 + h
         else:
             n = "abc".index(kind) * 2 + h
             src, dst = nsend.at[side, n], nrecv.at[side, n]
@@ -327,7 +329,8 @@
         k = far(side, dist)
         if kind == "d":
             got(("rs", side, "b", h))
-            value = acc[k, h] + nrecv[side, 2 + h].astype(F32)
+            got(("rs", side, "c", h))
+            value = acc[k, h] + nrecv[side, 2 + h].astype(F32) + nrecv[side, 4 + h].astype(F32)
             if h == half_of[side]:
                 got(("rs", side, "a", h))
                 value = value + nrecv[side, h].astype(F32)
@@ -337,12 +340,11 @@
         go(unit(side, kind, h))
         expect(("rs", side, kind, h), unit(side, kind, h))
 
-    pl.semaphore_wait(rdy.at[3], 2)
+    pl.semaphore_wait(rdy.at[4], 2)
     ready(0)
-    for side in range(2):
-        send_unit(side, "a", half_of[side])
-    for kind in ("b", "c"):
-        for h in (1, 0):
+    for h in (1, 0):
+        send_unit(half_of.index(h), "a", h)
+        for kind in ("b", "c"):
             for side in range(2):
                 send_unit(side, kind, h)
 
@@ -396,9 +398,6 @@
 
     for h in (1, 0):
         total = acc[z, h]
-        for side in range(2):
-            got(("rs", side, "c", h))
-            total = total + nrecv[side, 4 + h].astype(F32)
         for side in range(2):
             got(("rs", side, "d", h))
             total = total + rsb[side, h]
@@ -503,7 +502,7 @@
             pltpu.VMEM((4, 288, 256), BF16),
             pltpu.VMEM((4, 64, 512), BF16),
             pltpu.VMEM((4, 64, 512), BF16),
-            pltpu.VMEM((256, 2048), BF16),
+            pltpu.VMEM((192, 2048), BF16),
             pltpu.VMEM((8, 2, 216, 128), F32),
             pltpu.VMEM((2, 2, 216, 128), F32),
             pltpu.VMEM((2, 6, 216, 128), BF16),
@@ -515,7 +514,7 @@
             pltpu.VMEM((128, 1, 128), F32),
             pltpu.VMEM((2, 1, 128), F32),
             dma((4,)),
-            pltpu.SemaphoreType.REGULAR((4,)),
+            pltpu.SemaphoreType.REGULAR((5,)),
             dma((10,)), dma((8,)),
             dma((4,)), dma((4,)),
             dma((2,)), dma((2,)),

time: 63.8 us -> 61.2 us (0.959)
  Pallas kernels: 60.8 us -> 58.6 us
    pallas_call x1, Pallas kernels: 60.8 us -> 58.6 us  [shards(): pl.pallas_call(kernel, name='adasum_step', out_shape=(pltpu.VMEM((2, 256,...]
where the time goes in v4:
time: 61.2 us; the launch traced here: 60.6 us
  Pallas kernels  58.6 us (96%)
  local copies, waits for them, and re-layouts  1.32 us (2%)
  between operations  0.64 us (1%)
    pallas_call x1, Pallas kernels, shards(): pl.pallas_call(kernel, name='adasum_step', out_shape=(pltpu.VMEM((2, 256,...  58.6 us
    unnamed x2, local copies, waits for them, and re-layouts  1.32 us

profile of v4, /device:TPU:8, one launch (start us, length us, event | category | flops | bytes accessed | tf_op | source)
XLA Modules:
  0.0 60.6 jit_solution(10306179380378991775)
XLA Ops:
  0.6 58.6 %adasum_step.1 = (bf16[2,256,256]{2,1,0:T(8,128)(2,1)S(1)}, f32[32,216]{1,0:T(8,128)S(1)}) custom-call(bf16[2,256,256]{2,1,0:T(8,128)(2,1)} %bitcast.8, bf16[2,256,256]{2,1,0:T(8,128)(2,1)} %bitcast.9, bf16[9,3,256,256]{3,2,1,0:T(8,128)(2,1)} %bitcast.7), custom_call_target="tpu_custom_call" | custom-call | tf_op jit(solution)/shard_map/adasum_step/pallas_call | solution.py:488
  59.2 0.7 %copy.7 = bf16[1,2,16,16,256]{4,3,2,1,0:T(8,128)(2,1)} copy(bf16[1,2,16,16,256]{4,3,2,1,0:T(8,128)(2,1)S(1)} %bitcast.5) | data formatting | bytes 524288
  59.9 0.6 %copy.8 = f32[216,32]{0,1:T(8,128)} copy(f32[216,32]{0,1:T(8,128)S(1)} %bitcast.6) | data formatting | bytes 55296

commit v5 on v4

--- a/solution.py
+++ b/solution.py
@@ -243,7 +243,7 @@
         q = lax.rem(x + NX - dx, NX)
         return rcopy(gts.at[q], gtall.at[q], gss.at[dx], grs.at[dx], (z * NX + q, rep))
 
-    for dx in (2, 1, 3):
+    for dx in (1, 3, 2):
         go(g_send(dx))
         expect(("g", dx), g_recv(dx))
     gtall[x] = gts[x]

time: 61.2 us -> 61.3 us (level)
  no operation moved by 1% of the time
where the time goes in v5:
time: 61.3 us; the launch traced here: 60.5 us
  Pallas kernels  58.6 us (96%)
  local copies, waits for them, and re-layouts  1.32 us (2%)
  between operations  0.64 us (1%)
    pallas_call x1, Pallas kernels, shards(): pl.pallas_call(kernel, name='adasum_step', out_shape=(pltpu.VMEM((2, 256,...  58.6 us
    unnamed x2, local copies, waits for them, and re-layouts  1.32 us

profile of v5, /device:TPU:8, one launch (start us, length us, event | category | flops | bytes accessed | tf_op | source)
XLA Modules:
  0.0 60.5 jit_solution(3698709868947199946)
XLA Ops:
  0.6 58.6 %adasum_step.1 = (bf16[2,256,256]{2,1,0:T(8,128)(2,1)S(1)}, f32[32,216]{1,0:T(8,128)S(1)}) custom-call(bf16[2,256,256]{2,1,0:T(8,128)(2,1)} %bitcast.8, bf16[2,256,256]{2,1,0:T(8,128)(2,1)} %bitcast.9, bf16[9,3,256,256]{3,2,1,0:T(8,128)(2,1)} %bitcast.7), custom_call_target="tpu_custom_call" | custom-call | tf_op jit(solution)/shard_map/adasum_step/pallas_call | solution.py:488
  59.2 0.7 %copy.7 = bf16[1,2,16,16,256]{4,3,2,1,0:T(8,128)(2,1)} copy(bf16[1,2,16,16,256]{4,3,2,1,0:T(8,128)(2,1)S(1)} %bitcast.5) | data formatting | bytes 524288
  59.9 0.6 %copy.8 = f32[216,32]{0,1:T(8,128)} copy(f32[216,32]{0,1:T(8,128)S(1)} %bitcast.6) | data formatting | bytes 55296
